TPU v7x, 32 devices: a whole 2x2x4 slice. The times are simulated.
32 devices in a mesh: parts: 2 (over y), dp: 4 (over z), tensor: 4 (over x, core).
Axes of the slice: x: 2, y: 2, z: 4, core: 2. Of those that a mesh axis runs over, the one named last changes fastest.
Arguments:
- prompt_kv: bfloat16 [2, 14336, 8, 128], P(None, ('parts', 'dp'), 'tensor'), parts along dimension 1, may hold values from -12 to 12
- gen_kv: bfloat16 [64, 2, 128, 8, 128], P(('parts', 'dp'), None, None, 'tensor'), parts along dimension 0, may hold values from -17 to 17
- queries: bfloat16 [2, 64, 64, 128], P(None, ('parts', 'dp'), 'tensor'), parts along dimension 1, may hold values from -24 to 24
- new_kv: bfloat16 [2, 2, 64, 8, 128], P(None, None, ('parts', 'dp'), 'tensor'), parts along dimension 2, may hold values from -48 to 48
- ancestors: int32 [64], P(('parts', 'dp')), parts along dimension 0, may hold values from 0 to 31, as said below
- prior_twist: float32 [64], P(('parts', 'dp')), parts along dimension 0, may hold values from -290 to 6
- twist_vec: float32 [64, 128], P('tensor'), may hold values from -1 to 1
Outputs:
- attended: bfloat16 [2, 64, 64, 128], P(None, ('parts', 'dp'), 'tensor'), parts along dimension 1
- log_weights: float32 [64], P(('parts', 'dp')), parts along dimension 0
There are 2 independent parts, one for each index of `parts`. A program takes and returns all parts, laid end to end along the dimension named above; an argument that names none is the same for every part. Nothing has to cross between parts.
Inputs may be any that keep to these rules, and one draw needn't show every extreme that they name: Duplicates are allowed. Among the 8 particles of one device (equal p // 8) at most 4 have ancestors held by one same device (equal ancestors // 8), and every device has exactly 4 from some device.
All inputs are finite; a program needn't handle non-finite values.
Results may differ from a plain program's by a relative error of at most 0.0017.
Values may be sent and summed in bfloat16 or wider, within the bound.
A program may use at most 128 MiB of HBM per device.

v0:
```python
import math
import jax
import jax.numpy as jnp
from jax import lax
from jax.sharding import PartitionSpec as P


def join_states(left_state, right_state):
    largest = jnp.maximum(left_state[0], right_state[0])
    left_scale = jnp.exp(left_state[0] - largest)
    right_scale = jnp.exp(right_state[0] - largest)
    return (
        largest,
        left_state[1] * left_scale + right_state[1] * right_scale,
        left_state[2] * left_scale[..., None] + right_state[2] * right_scale[..., None],
    )


def fold_blocks(moments, totals, weighted, along):
    largest = jnp.max(moments, axis=along)
    scale_each = jnp.exp(moments - jnp.expand_dims(largest, along))
    return (
        largest,
        jnp.sum(totals * scale_each, axis=along),
        jnp.sum(weighted * scale_each[..., None], axis=along),
    )


def block_state(scores, values, pattern):
    largest = jnp.max(scores, axis=-1)
    exponent = jnp.exp(scores - largest[..., None])
    weighted = jnp.einsum(
        pattern, exponent.astype(jnp.bfloat16), values, preferred_element_type=jnp.float32
    )
    return (largest, jnp.sum(exponent, axis=-1), weighted)


def prompt_states(query_rows, prompt_kv, kv_count, scaling):
    row_count, head_count, head_size = query_rows.shape
    group_size = head_count // kv_count
    per_block = math.gcd(row_count, 256)
    blocked = query_rows.reshape(row_count // per_block, per_block, kv_count, group_size, head_size)
    key_rows = prompt_kv[0]
    values = prompt_kv[1]

    def attend_block(query_block):
        scores = (
            jnp.einsum("pcgd,kcd->pcgk", query_block, key_rows, preferred_element_type=jnp.float32)
            * scaling
        )
        return block_state(scores, values, "pcgk,kcd->pcgd")

    largest, totals, weighted = lax.map(attend_block, blocked)
    return (
        largest.reshape(row_count, head_count),
        totals.reshape(row_count, head_count),
        weighted.reshape(row_count, head_count, head_size),
    )


def per_device(prompt_kv, gen_kv, queries, new_kv, ancestors, prior_twist, twist_vec):
    step_count, local_count, head_count, head_size = queries.shape
    kv_count = prompt_kv.shape[2]
    group_size = head_count // kv_count
    scaling = 1.0 / math.sqrt(head_size)
    devices = lax.axis_size("dp")
    capacity = max(2, (2 * local_count + devices - 1) // devices)
    slot_total = devices * capacity
    source = ancestors // local_count
    offset = ancestors % local_count
    places = jnp.arange(local_count)
    earlier = (source[:, None] == source[None, :]) & (places[None, :] < places[:, None])
    arrival_rank = jnp.sum(earlier.astype(jnp.int32), axis=1)
    slot_index = source * capacity + arrival_rank
    slot_match = jnp.arange(slot_total)[:, None] == slot_index[None, :]
    wanted = jnp.sum(jnp.where(slot_match, offset[None, :] + 1, 0), axis=1) - 1
    requests_in = lax.all_to_all(
        wanted.reshape(devices, capacity), "dp", split_axis=0, concat_axis=0, tiled=True
    )
    picked = jnp.clip(requests_in, 0, local_count - 1).reshape(-1)
    every_prior = lax.all_gather(prior_twist, "dp", axis=0, tiled=True)
    twist_before = jnp.take(every_prior, ancestors, axis=0)
    split_query = queries.reshape(step_count, local_count, kv_count, group_size, head_size)
    sent_rows = jnp.take(gen_kv, picked, axis=0).reshape((devices, capacity) + gen_kv.shape[1:])
    arrived = lax.all_to_all(sent_rows, "dp", split_axis=0, concat_axis=0, tiled=True)
    resampled = jnp.take(arrived.reshape((slot_total,) + gen_kv.shape[1:]), slot_index, axis=0)
    cache_scores = (
        jnp.einsum(
            "spcgd,pkcd->spcgk", split_query, resampled[:, 0], preferred_element_type=jnp.float32
        )
        * scaling
    )
    largest, totals, weighted = block_state(cache_scores, resampled[:, 1], "spcgk,pkcd->spcgd")
    cached = (
        largest.reshape(step_count, local_count, head_count),
        totals.reshape(step_count, local_count, head_count),
        weighted.reshape(step_count, local_count, head_count, head_size),
    )
    new_scores = (
        jnp.einsum(
            "spcgd,tpcd->spcgt", split_query, new_kv[:, 0], preferred_element_type=jnp.float32
        )
        * scaling
    )
    positions = jnp.arange(step_count)
    allowed = positions[None, :] <= positions[:, None]
    new_scores = jnp.where(allowed[:, None, None, None, :], new_scores, -jnp.inf)
    largest, totals, weighted = block_state(new_scores, new_kv[:, 1], "spcgt,tpcd->spcgd")
    fresh_state = (
        largest.reshape(step_count, local_count, head_count),
        totals.reshape(step_count, local_count, head_count),
        weighted.reshape(step_count, local_count, head_count, head_size),
    )
    everyone = lax.all_gather(queries, "dp", axis=1, tiled=True)
    largest, totals, weighted = prompt_states(
        everyone.reshape(step_count * devices * local_count, head_count, head_size),
        prompt_kv,
        kv_count,
        scaling,
    )
    arrived_states = (
        lax.all_to_all(
            largest.reshape(step_count, devices, local_count, head_count),
            "dp",
            split_axis=1,
            concat_axis=1,
            tiled=True,
        ),
        lax.all_to_all(
            totals.reshape(step_count, devices, local_count, head_count),
            "dp",
            split_axis=1,
            concat_axis=1,
            tiled=True,
        ),
        lax.all_to_all(
            weighted.reshape(step_count, devices, local_count, head_count, head_size),
            "dp",
            split_axis=1,
            concat_axis=1,
            tiled=True,
        ),
    )
    prompt_state = fold_blocks(arrived_states[0], arrived_states[1], arrived_states[2], 1)
    joined = join_states(join_states(prompt_state, cached), fresh_state)
    attended = (joined[2] / joined[1][..., None]).astype(jnp.bfloat16)
    last_step = lax.optimization_barrier(attended[-1]).astype(jnp.float32)
    local_twist = jnp.sum(last_step * twist_vec, axis=(1, 2))
    twist_value = lax.psum(local_twist, "tensor")
    raw_weight = twist_value - twist_before
    largest_weight = lax.pmax(jnp.max(raw_weight), "dp")
    weight_mass = lax.psum(jnp.sum(jnp.exp(raw_weight - largest_weight)), "dp")
    normalizer = largest_weight + jnp.log(weight_mass)
    return (attended, raw_weight - normalizer)


def solution(mesh):
    placed = (
        P(None, ("parts", "dp"), "tensor", None),
        P(("parts", "dp"), None, None, "tensor", None),
        P(None, ("parts", "dp"), "tensor", None),
        P(None, None, ("parts", "dp"), "tensor", None),
        P(("parts", "dp")),
        P(("parts", "dp")),
        P("tensor", None),
    )
    return jax.shard_map(
        per_device,
        mesh=mesh,
        in_specs=placed,
        out_specs=(P(None, ("parts", "dp"), "tensor", None), P(("parts", "dp"))),
        check_vma=False,
    )
```

profile of v0, /device:TPU:0, one launch (start us, length us, event | category | flops | bytes accessed | tf_op | source)
XLA Modules:
  0.0 157.3 jit_solution(7130623179860953342)
XLA Ops:
  0.6 0.8 compare_select_fusion.3
  1.4 0.2 convert_reduce_fusion
  1.7 0.7 sub.106
  2.4 6.3 %all-to-all-start.2 = ((s32[4,1,4]{2,1,0:T(1,128)}), s32[4,1,4]{2,1,0:T(1,128)S(1)}, u32[]{:S(2)}, u32[]{:S(2)}) async-start(s32[4,1,4]{2,1,0:T(1,128)} %bitcast.10), calls=%async_computation.2 | async-start | bytes 4096 | tf_op jit(solution)/shard_map/all_to_all | solution.py:77
  8.7 14.6 %all_gather.6 = bf16[2,32,16,128]{3,2,1,0:T(8,128)(2,1)S(1)} all-gather(bf16[2,8,16,128]{3,2,1,0:T(8,128)(2,1)} %param.9), channel_id=1, replica_groups=mesh['parts'=2,'dp'=4,'tensor'=4] {'dp'}, dimensions={1}, use_global_device_ids=true | all-gather | bytes 327680 | tf_op jit(solution)/shard_map/all_gather | solution.py:114
  23.4 2.5 %fusion.38 = (bf16[1,1792,2,128]{3,2,1,0:T(2,128)(2,1)S(1)}, bf16[1,1792,2,128]{3,2,1,0:T(2,128)(2,1)S(1)}) fusion(bf16[2,1792,2,128]{3,2,1,0:T(2,128)(2,1)} %param.7), kind=kLoop, calls=%fused_computation.88 | loop fusion | bytes 3670016 | tf_op jit(solution)/shard_map/slice | solution.py:44
  25.9 4.1 %bitcast_reduce_fusion = (f32[64,2,8]{0,2,1:T(8,128)S(1)}, f32[2,1792,64,8]{1,2,3,0:T(8,128)}) fusion(bf16[64,2,8,128]{3,0,2,1:T(8,128)(2,1)S(1)} %bitcast.113, bf16[1,1792,2,128]{3,2,1,0:T(2,128)(2,1)S(1)} %get-tuple-element.35), kind=kOutput, calls=%fused_computation.4 | convolution fusion | flops 473431040 | bytes 8523776 | tf_op jit(solution)/shard_map/while/body/eval_jaxpr/pcgd,kcd->pcgk/dot_general | solution.py:48
  30.0 0.1 reshape_reshape.11
  30.1 0.1 copy.105
  30.2 4.4 %fusion.3 = f32[2,64,8,128]{3,1,2,0:T(8,128)S(1)} fusion(f32[2,1792,64,8]{1,2,3,0:T(8,128)} %get-tuple-element.48, f32[64,2,8]{0,2,1:T(8,128)S(1)} %get-tuple-element.47, bf16[1,1792,2,128]{3,2,1,0:T(2,128)(2,1)S(1)} %get-tuple-element.34), kind=kOutput, calls=%fused_computation.8 | convolution fusion | flops 475267072 | bytes 8785920 | tf_op jit(solution)/shard_map/while/body/eval_jaxpr/pcgk,kcd->pcgd/dot_general | solution.py:32
  34.6 0.7 reshape.241
  35.3 4.9 %all-to-all-start.1 = ((f32[4,1,256]{2,1,0:T(1,128)}), f32[4,1,256]{2,1,0:T(1,128)S(1)}, u32[]{:S(2)}, u32[]{:S(2)}) async-start(f32[4,1,256]{2,1,0:T(1,128)} %reshape.241), calls=%async_computation.1 | async-start | bytes 8192 | tf_op jit(solution)/shard_map/all_to_all | solution.py:122
  40.2 4.4 %fusion.1 = f32[64,2,8]{0,2,1:T(8,128)S(1)} fusion(f32[2,1792,64,8]{1,2,3,0:T(8,128)} %get-tuple-element.48, f32[64,2,8]{0,2,1:T(8,128)S(1)} %get-tuple-element.47), kind=kLoop, calls=%fused_computation.6 | loop fusion | flops 5504000 | bytes 7348224 | tf_op jit(solution)/shard_map/while/body/eval_jaxpr/reduce_sum | solution.py:35
  44.6 1.1 copy.104
  45.7 0.1 reshape_reshape.12
  45.8 0.1 copy.121
  45.9 0.7 reshape.243
  46.6 5.1 %all-to-all-start.4 = ((f32[4,1,256]{2,1,0:T(1,128)}), f32[4,1,256]{2,1,0:T(1,128)S(1)}, u32[]{:S(2)}, u32[]{:S(2)}) async-start(f32[4,1,256]{2,1,0:T(1,128)} %reshape.243), calls=%async_computation.4 | async-start | bytes 8192 | tf_op jit(solution)/shard_map/all_to_all | solution.py:129
  51.8 5.5 %all-to-all-done.4 = f32[4,1,256]{2,1,0:T(1,128)S(1)} async-done(((f32[4,1,256]{2,1,0:T(1,128)}), f32[4,1,256]{2,1,0:T(1,128)S(1)}, u32[]{:S(2)}, u32[]{:S(2)}) %all-to-all-start.4) | async-done | bytes 4128 | tf_op jit(solution)/shard_map/all_to_all | solution.py:129
  57.3 4.1 %all-to-all-start = ((f32[2,4,8,16,128]{4,3,2,0,1:T(8,128)}), f32[2,4,8,16,128]{4,3,2,0,1:T(8,128)}, u32[]{:S(2)}, u32[]{:S(2)}) async-start(f32[2,4,8,16,128]{4,3,2,0,1:T(8,128)} %copy.104), calls=%async_computation | async-start | bytes 1048576 | tf_op jit(solution)/shard_map/all_to_all | solution.py:136
  61.4 5.1 %gather_fusion = bf16[16,2,128,2,128]{4,3,2,1,0:T(2,128)(2,1)S(1)} fusion(bf16[8,2,128,2,128]{4,3,2,1,0:T(2,128)(2,1)S(1)} %copy-done, s32[1024]{0:T(1024)S(1)} %pad_clamp_fusion.2), kind=kCustom, calls=%fused_computation | custom fusion | bytes 4194368 | tf_op jit(solution)/shard_map/jit(_take)/gather | solution.py:84
  66.5 1.7 %copy_select_fusion = bf16[4,4,2,128,2,128]{5,3,4,2,1,0:T(8,128)(2,1)} fusion(bf16[4,4,2,128,2,128]{5,4,3,2,1,0:T(2,128)(2,1)S(1)} %bitcast.110, pred[4,4]{1,0:T(4,128)(4,1)S(1)} %compare_and_fusion), kind=kLoop, calls=%fused_computation.11 | loop fusion | flops 1048576 | bytes 4194320 | tf_op jit(solution)/shard_map/jit(_take)/select_n | solution.py:84
  68.2 3.6 %all-to-all-done = f32[2,4,8,16,128]{4,3,2,0,1:T(8,128)} async-done(((f32[2,4,8,16,128]{4,3,2,0,1:T(8,128)}), f32[2,4,8,16,128]{4,3,2,0,1:T(8,128)}, u32[]{:S(2)}, u32[]{:S(2)}) %all-to-all-start) | async-done | bytes 524320 | tf_op jit(solution)/shard_map/all_to_all | solution.py:136
  71.9 3.6 %all-to-all-start.3 = ((bf16[4,4,2,128,2,128]{5,3,4,2,1,0:T(8,128)(2,1)}), bf16[4,4,2,128,2,128]{5,3,4,2,1,0:T(8,128)(2,1)S(1)}, u32[]{:S(2)}, u32[]{:S(2)}) async-start(bf16[4,4,2,128,2,128]{5,3,4,2,1,0:T(8,128)(2,1)} %copy_select_fusion), calls=%async_computation.3 | async-start | bytes 4194304 | tf_op jit(solution)/shard_map/all_to_all | solution.py:85
  75.5 0.4 fusion.40
  76.2 0.6 dynamic-slice
  77.5 0.2 dynamic-update-slice
  77.7 31.2 %all-reduce = f32[32]{0:T(128)S(1)} all-reduce(f32[32]{0:T(128)S(1)} %dynamic-update-slice), channel_id=1, replica_groups=mesh['parts'=2,'dp'=4,'tensor'=4] {'dp'}, use_global_device_ids=true, to_apply=%add | all-reduce | flops 32 | bytes 256
  109.0 0.2 convolution_bitcast_fusion.1
  109.2 0.5 broadcast.204
  109.7 0.7 reduce.4
  110.4 0.7 reduce.5
  111.2 1.3 multiply_reduce_fusion
  112.5 4.7 %all-to-all-done.3 = bf16[4,4,2,128,2,128]{5,3,4,2,1,0:T(8,128)(2,1)S(1)} async-done(((bf16[4,4,2,128,2,128]{5,3,4,2,1,0:T(8,128)(2,1)}), bf16[4,4,2,128,2,128]{5,3,4,2,1,0:T(8,128)(2,1)S(1)}, u32[]{:S(2)}, u32[]{:S(2)}) %all-to-all-start.3) | async-done | bytes 2097184 | tf_op jit(solution)/shard_map/all_to_all | solution.py:85
  117.2 1.7 %gather_fusion.1 = bf16[8,2,128,2,128]{4,2,3,1,0:T(8,128)(2,1)} fusion(bf16[16,2,128,2,128]{4,2,3,1,0:T(8,128)(2,1)S(1)} %bitcast.111, s32[1024]{0:T(1024)S(1)} %pad_clamp_fusion.1), kind=kCustom, calls=%fused_computation.1 | custom fusion | bytes 2097184 | tf_op jit(solution)/shard_map/jit(_take)/gather | solution.py:86
  118.9 1.4 copy_select_fusion.1
  120.3 0.5 fusion.41
  120.8 0.3 convolution_bitcast_fusion
  121.1 0.2 fusion.16
  121.5 0.2 fusion.13
  121.8 0.1 multiply_reduce_fusion.1
  121.9 0.6 gather_fusion.2
  122.6 5.7 %psum.14 = f32[8]{0:T(128)S(1)} all-reduce(f32[8]{0:T(128)S(1)} %multiply_reduce_fusion.1), channel_id=1, replica_groups=mesh['parts'=2,'dp'=4,'tensor'=4] {'tensor'}, use_global_device_ids=true, to_apply=%region_12.13 | all-reduce | flops 8 | bytes 64 | tf_op jit(solution)/shard_map/psum | solution.py:149
  128.2 0.6 fusion.34
  128.8 16.2 %pmax.7 = f32[]{:T(128)} all-reduce(f32[]{:T(128)} %get-tuple-element.16), channel_id=1, replica_groups=mesh['parts'=2,'dp'=4,'tensor'=4] {'dp'}, use_global_device_ids=true, to_apply=%region_14.15 | all-reduce | flops 1 | bytes 8 | tf_op jit(solution)/shard_map/pmax | solution.py:151
  145.0 1.3 exponential_reduce_fusion
  146.3 9.1 %psum.15 = f32[]{:T(128)} all-reduce(f32[]{:T(128)} %exponential_reduce_fusion), channel_id=1, replica_groups=mesh['parts'=2,'dp'=4,'tensor'=4] {'dp'}, use_global_device_ids=true, to_apply=%region_16.17 | all-reduce | flops 1 | bytes 8 | tf_op jit(solution)/shard_map/psum | solution.py:152
  156.8 0.5 broadcast_subtract_fusion
  (48 shorter events, 1.0 us)
Async XLA Ops:
  0.6 60.8 %copy-start = (bf16[8,2,128,2,128]{4,3,2,1,0:T(2,128)(2,1)S(1)}, bf16[8,2,128,2,128]{4,3,2,1,0:T(2,128)(2,1)}, u32[]{:S(2)}) copy-start(bf16[8,2,128,2,128]{4,3,2,1,0:T(2,128)(2,1)} %param.8) | copy-start | bytes 3145732
  2.4 32.9 %all-to-all-start.2 = ((s32[4,1,4]{2,1,0:T(1,128)}), s32[4,1,4]{2,1,0:T(1,128)S(1)}, u32[]{:S(2)}, u32[]{:S(2)}) async-start(s32[4,1,4]{2,1,0:T(1,128)} %bitcast.10), calls=%async_computation.2 | async-start | bytes 4096 | tf_op jit(solution)/shard_map/all_to_all | solution.py:77
  35.3 11.3 %all-to-all-start.1 = ((f32[4,1,256]{2,1,0:T(1,128)}), f32[4,1,256]{2,1,0:T(1,128)S(1)}, u32[]{:S(2)}, u32[]{:S(2)}) async-start(f32[4,1,256]{2,1,0:T(1,128)} %reshape.241), calls=%async_computation.1 | async-start | bytes 8192 | tf_op jit(solution)/shard_map/all_to_all | solution.py:122
  44.6 30.9 %copy-start.3 = (bf16[2,2,8,2,128]{4,3,2,1,0:T(2,128)(2,1)S(1)}, bf16[2,2,8,2,128]{4,3,2,1,0:T(2,128)(2,1)}, u32[]{:S(2)}) copy-start(bf16[2,2,8,2,128]{4,3,2,1,0:T(2,128)(2,1)} %param.10) | copy-start | bytes 49156
  44.6 30.9 %copy-start.2 = (bf16[2,8,16,128]{3,2,1,0:T(8,128)(2,1)S(1)}, bf16[2,8,16,128]{3,2,1,0:T(8,128)(2,1)}, u32[]{:S(2)}) copy-start(bf16[2,8,16,128]{3,2,1,0:T(8,128)(2,1)} %param.9) | copy-start | bytes 196612
  45.7 30.5 %copy-start.7 = (u32[32]{0:T(128)S(1)}, u32[32]{0:T(128)}, u32[]{:S(2)}) copy-start(u32[32]{0:T(128)} %constant.108) | copy-start | bytes 388
  45.7 31.8 %copy-start.6 = (f32[8]{0:T(128)S(1)}, f32[8]{0:T(128)}, u32[]{:S(2)}) copy-start(f32[8]{0:T(128)} %param.12) | copy-start | bytes 100
  46.6 10.7 %all-to-all-start.4 = ((f32[4,1,256]{2,1,0:T(1,128)}), f32[4,1,256]{2,1,0:T(1,128)S(1)}, u32[]{:S(2)}, u32[]{:S(2)}) async-start(f32[4,1,256]{2,1,0:T(1,128)} %reshape.243), calls=%async_computation.4 | async-start | bytes 8192 | tf_op jit(solution)/shard_map/all_to_all | solution.py:129
  57.3 14.6 %all-to-all-start = ((f32[2,4,8,16,128]{4,3,2,0,1:T(8,128)}), f32[2,4,8,16,128]{4,3,2,0,1:T(8,128)}, u32[]{:S(2)}, u32[]{:S(2)}) async-start(f32[2,4,8,16,128]{4,3,2,0,1:T(8,128)} %copy.104), calls=%async_computation | async-start | bytes 1048576 | tf_op jit(solution)/shard_map/all_to_all | solution.py:136
  68.2 53.6 %copy-start.4 = (f32[16,128]{1,0:T(8,128)S(1)}, f32[16,128]{1,0:T(8,128)}, u32[]{:S(2)}) copy-start(f32[16,128]{1,0:T(8,128)} %param.13) | copy-start | bytes 24580
  68.2 60.0 %copy-start.5 = (s32[8]{0:T(128)S(1)}, s32[8]{0:T(128)}, u32[]{:S(2)}) copy-start(s32[8]{0:T(128)} %param.11) | copy-start | bytes 100
  71.9 45.4 %all-to-all-start.3 = ((bf16[4,4,2,128,2,128]{5,3,4,2,1,0:T(8,128)(2,1)}), bf16[4,4,2,128,2,128]{5,3,4,2,1,0:T(8,128)(2,1)S(1)}, u32[]{:S(2)}, u32[]{:S(2)}) async-start(bf16[4,4,2,128,2,128]{5,3,4,2,1,0:T(8,128)(2,1)} %copy_select_fusion), calls=%async_computation.3 | async-start | bytes 4194304 | tf_op jit(solution)/shard_map/all_to_all | solution.py:85
  121.8 35.5 %copy-start.1 = (bf16[2,8,16,128]{3,2,1,0:T(8,128)(2,1)}, bf16[2,8,16,128]{3,2,1,0:T(8,128)(2,1)S(1)}, u32[]{:S(2)}) copy-start(bf16[2,8,16,128]{3,2,1,0:T(8,128)(2,1)S(1)} %fusion.13) | copy-start | bytes 196612
where the time goes:
time: 158 us; the launch traced here: 157 us
  blocking collectives  76.7 us (49%)
  starting transfers between devices  24 us (15%)
  local copies, waits for them, and re-layouts  15.5 us (10%)
  other arithmetic  14.3 us (9%)
  waiting for transfers between devices  13.8 us (9%)
  matrix products  9.94 us (6%)
  between operations  2.94 us (2%)
    unnamed x1, blocking collectives  31.2 us
    pmax x1, blocking collectives, per_device(): largest_weight = lax.pmax(jnp.max(raw_weight), 'dp')  16.2 us
    all_gather x1, blocking collectives, per_device(): everyone = lax.all_gather(queries, 'dp', axis=1, tiled=True)  14.6 us
    psum x1, blocking collectives, per_device(): weight_mass = lax.psum(jnp.sum(jnp.exp(raw_weight - largest_weight)), 'dp')  9.05 us
    all_to_all x1, starting transfers between devices, per_device(): lax.all_to_all(wanted.reshape(devices, capacity), 'dp', split_axis=0, con...  6.35 us
    psum x1, blocking collectives, per_device(): twist_value = lax.psum(local_twist, 'tensor')  5.66 us
    all_to_all x1, waiting for transfers between devices, per_device(): lax.all_to_all(totals.reshape(step_count, devices, local_count, head_coun...  5.47 us
    all_to_all x1, starting transfers between devices, per_device(): lax.all_to_all(totals.reshape(step_count, devices, local_count, head_coun...  5.09 us
  transfers between devices with their start and end apart: 5, of which 3 were waited for; matrix products, arithmetic and copies ran while one was open for 19% of the time, Pallas kernels for 0%

commit v1 on v0

--- a/solution.py
+++ b/solution.py
@@ -3,6 +3,29 @@
 import jax.numpy as jnp
 from jax import lax
 from jax.sharding import PartitionSpec as P
+
+
+def in_blocks(array, dim, devices):
+    shape = array.shape
+    parts = array.reshape(*shape[:dim], devices, shape[dim] // devices, *shape[dim + 1 :])
+    return jnp.moveaxis(parts, dim, 0)
+
+
+def laid_out(blocks, dim):
+    blocks = jnp.moveaxis(blocks, 0, dim)
+    shape = blocks.shape
+    return blocks.reshape(*shape[:dim], shape[dim] * shape[dim + 1], *shape[dim + 2 :])
+
+
+def swapped_with_each(shard, axis, split_dim, concat_dim):
+    size, position = (lax.axis_size(axis), lax.axis_index(axis))
+    tiles = in_blocks(shard, split_dim, size)
+    outs = [tiles[position]]
+    for step in range(1, size):
+        sent = tiles[position ^ step]
+        outs.append(lax.ppermute(sent, axis, [(i, i ^ step) for i in range(size)]))
+    tiles = jnp.stack(outs)[position ^ jnp.arange(size)]
+    return laid_out(tiles, concat_dim)
 
 
 def join_states(left_state, right_state):
@@ -126,13 +149,7 @@
             concat_axis=1,
             tiled=True,
         ),
-        lax.all_to_all(
-            totals.reshape(step_count, devices, local_count, head_count),
-            "dp",
-            split_axis=1,
-            concat_axis=1,
-            tiled=True,
-        ),
+        swapped_with_each(totals.reshape(step_count, devices, local_count, head_count), "dp", 1, 1),
         lax.all_to_all(
             weighted.reshape(step_count, devices, local_count, head_count, head_size),
             "dp",

time: 158 us -> 148 us (0.937)
  blocking collectives: 76.7 us -> 64.8 us
  waiting for transfers between devices: 13.8 us -> 17.3 us
    unnamed x1, blocking collectives: 31.2 us -> 22.8 us
    ppermute x0 -> x3, waiting for transfers between devices: none -> 8.38 us  [swapped_with_each(): outs.append(lax.ppermute(sent, axis, [(i, i ^ step) for i in range(size)]))]
    all_to_all x1 -> x0, waiting for transfers between devices: 5.47 us -> none  [per_device(): lax.all_to_all(totals.reshape(step_count, devices, local_count, head_coun...]
    all_to_all x1, waiting for transfers between devices: 0.01 us -> 5.47 us  [per_device(): lax.all_to_all(largest.reshape(step_count, devices, local_count, head_cou...]
    all_to_all x1 -> x0, starting transfers between devices: 5.09 us -> none  [per_device(): lax.all_to_all(totals.reshape(step_count, devices, local_count, head_coun...]
    all_to_all x1, waiting for transfers between devices: 4.73 us -> 0.01 us  [per_device(): lax.all_to_all(sent_rows, 'dp', split_axis=0, concat_axis=0, tiled=True)]
    ppermute x0 -> x3, starting transfers between devices: none -> 4.39 us  [swapped_with_each(): outs.append(lax.ppermute(sent, axis, [(i, i ^ step) for i in range(size)]))]
    pmax x1, blocking collectives: 16.2 us -> 12.7 us  [per_device(): largest_weight = lax.pmax(jnp.max(raw_weight), 'dp')]
  transfers between devices with their start and end apart: 5 -> 7, of which waited for: 3 -> 3; matrix products, arithmetic and copies ran while one was open for 19% -> 20% of each run, Pallas kernels for 0% -> 0%
where the time goes in v1:
time: 148 us
  blocking collectives  64.8 us (44%)
  starting transfers between devices  23.4 us (16%)
  waiting for transfers between devices  17.3 us (12%)
  local copies, waits for them, and re-layouts  15.5 us (10%)
  other arithmetic  13.7 us (9%)
  matrix products  9.95 us (7%)
  between operations  3.05 us (2%)
    unnamed x1, blocking collectives  22.8 us
    all_gather x1, blocking collectives, per_device(): everyone = lax.all_gather(queries, 'dp', axis=1, tiled=True)  14.6 us
    pmax x1, blocking collectives, per_device(): largest_weight = lax.pmax(jnp.max(raw_weight), 'dp')  12.7 us
    psum x1, blocking collectives, per_device(): weight_mass = lax.psum(jnp.sum(jnp.exp(raw_weight - largest_weight)), 'dp')  9.05 us
    ppermute x3, waiting for transfers between devices, swapped_with_each(): outs.append(lax.ppermute(sent, axis, [(i, i ^ step) for i in range(size)]))  8.38 us
    all_to_all x1, starting transfers between devices, per_device(): lax.all_to_all(wanted.reshape(devices, capacity), 'dp', split_axis=0, con...  6.35 us
    psum x1, blocking collectives, per_device(): twist_value = lax.psum(local_twist, 'tensor')  5.66 us
    all_to_all x1, waiting for transfers between devices, per_device(): lax.all_to_all(largest.reshape(step_count, devices, local_count, head_cou...  5.47 us
  transfers between devices with their start and end apart: 7, of which 3 were waited for; matrix products, arithmetic and copies ran while one was open for 20% of the time, Pallas kernels for 0%

profile of v1, /device:TPU:0, one launch (start us, length us, event | category | flops | bytes accessed | tf_op | source)
XLA Modules:
  0.0 147.7 jit_solution(11730348364155917473)
XLA Ops:
  0.6 0.8 compare_select_fusion.4
  1.4 0.2 convert_reduce_fusion
  1.6 0.1 select_reduce_fusion
  1.7 0.7 sub.106
  2.4 6.3 %all-to-all-start.2 = ((s32[4,1,4]{2,1,0:T(1,128)}), s32[4,1,4]{2,1,0:T(1,128)S(1)}, u32[]{:S(2)}, u32[]{:S(2)}) async-start(s32[4,1,4]{2,1,0:T(1,128)} %bitcast.10), calls=%async_computation.2 | async-start | bytes 4096 | tf_op jit(solution)/shard_map/all_to_all | solution.py:100
  8.7 14.6 %all_gather.6 = bf16[2,32,16,128]{3,2,1,0:T(8,128)(2,1)S(1)} all-gather(bf16[2,8,16,128]{3,2,1,0:T(8,128)(2,1)} %param.9), channel_id=1, replica_groups=mesh['parts'=2,'dp'=4,'tensor'=4] {'dp'}, dimensions={1}, use_global_device_ids=true | all-gather | bytes 327680 | tf_op jit(solution)/shard_map/all_gather | solution.py:137
  23.4 2.5 %fusion.40 = (bf16[1,1792,2,128]{3,2,1,0:T(2,128)(2,1)S(1)}, bf16[1,1792,2,128]{3,2,1,0:T(2,128)(2,1)S(1)}) fusion(bf16[2,1792,2,128]{3,2,1,0:T(2,128)(2,1)} %param.7), kind=kLoop, calls=%fused_computation.98 | loop fusion | bytes 3670016 | tf_op jit(solution)/shard_map/slice | solution.py:67
  25.9 4.1 %bitcast_reduce_fusion = (f32[64,2,8]{0,2,1:T(8,128)S(1)}, f32[2,1792,64,8]{1,2,3,0:T(8,128)}) fusion(bf16[64,2,8,128]{3,0,2,1:T(8,128)(2,1)S(1)} %bitcast.129, bf16[1,1792,2,128]{3,2,1,0:T(2,128)(2,1)S(1)} %get-tuple-element.35), kind=kOutput, calls=%fused_computation.5 | convolution fusion | flops 473431040 | bytes 8523776 | tf_op jit(solution)/shard_map/while/body/eval_jaxpr/pcgd,kcd->pcgk/dot_general | solution.py:71
  30.0 0.1 reshape_reshape.8
  30.1 4.4 %fusion.3 = f32[2,64,8,128]{3,1,2,0:T(8,128)S(1)} fusion(f32[2,1792,64,8]{1,2,3,0:T(8,128)} %get-tuple-element.52, f32[64,2,8]{0,2,1:T(8,128)S(1)} %get-tuple-element.51, bf16[1,1792,2,128]{3,2,1,0:T(2,128)(2,1)S(1)} %get-tuple-element.34), kind=kOutput, calls=%fused_computation.9 | convolution fusion | flops 475267072 | bytes 8785920 | tf_op jit(solution)/shard_map/while/body/eval_jaxpr/pcgk,kcd->pcgd/dot_general | solution.py:55
  34.5 1.1 copy.88
  35.6 0.1 copy.89
  35.7 0.7 reshape.278
  36.4 4.9 %all-to-all-start.1 = ((f32[4,1,256]{2,1,0:T(1,128)}), f32[4,1,256]{2,1,0:T(1,128)S(1)}, u32[]{:S(2)}, u32[]{:S(2)}) async-start(f32[4,1,256]{2,1,0:T(1,128)} %reshape.278), calls=%async_computation.1 | async-start | bytes 8192 | tf_op jit(solution)/shard_map/all_to_all | solution.py:145
  41.4 5.5 %all-to-all-done.1 = f32[4,1,256]{2,1,0:T(1,128)S(1)} async-done(((f32[4,1,256]{2,1,0:T(1,128)}), f32[4,1,256]{2,1,0:T(1,128)S(1)}, u32[]{:S(2)}, u32[]{:S(2)}) %all-to-all-start.1) | async-done | bytes 4128 | tf_op jit(solution)/shard_map/all_to_all | solution.py:145
  46.9 4.1 %all-to-all-start = ((f32[2,4,8,16,128]{4,3,2,0,1:T(8,128)}), f32[2,4,8,16,128]{4,3,2,0,1:T(8,128)}, u32[]{:S(2)}, u32[]{:S(2)}) async-start(f32[2,4,8,16,128]{4,3,2,0,1:T(8,128)} %copy.88), calls=%async_computation | async-start | bytes 1048576 | tf_op jit(solution)/shard_map/all_to_all | solution.py:153
  51.1 5.1 %gather_fusion = bf16[16,2,128,2,128]{4,3,2,1,0:T(2,128)(2,1)S(1)} fusion(bf16[8,2,128,2,128]{4,3,2,1,0:T(2,128)(2,1)S(1)} %copy-done, s32[1024]{0:T(1024)S(1)} %pad_clamp_fusion.3), kind=kCustom, calls=%fused_computation | custom fusion | bytes 4194368 | tf_op jit(solution)/shard_map/jit(_take)/gather | solution.py:107
  56.2 1.7 %copy_select_fusion = bf16[4,4,2,128,2,128]{5,3,4,2,1,0:T(8,128)(2,1)} fusion(bf16[4,4,2,128,2,128]{5,4,3,2,1,0:T(2,128)(2,1)S(1)} %bitcast.126, pred[4,4]{1,0:T(4,128)(4,1)S(1)} %compare_and_fusion), kind=kLoop, calls=%fused_computation.12 | loop fusion | flops 1048576 | bytes 4194320 | tf_op jit(solution)/shard_map/jit(_take)/select_n | solution.py:107
  57.9 3.5 %all-to-all-done = f32[2,4,8,16,128]{4,3,2,0,1:T(8,128)} async-done(((f32[2,4,8,16,128]{4,3,2,0,1:T(8,128)}), f32[2,4,8,16,128]{4,3,2,0,1:T(8,128)}, u32[]{:S(2)}, u32[]{:S(2)}) %all-to-all-start) | async-done | bytes 524320 | tf_op jit(solution)/shard_map/all_to_all | solution.py:153
  61.4 3.6 %all-to-all-start.3 = ((bf16[4,4,2,128,2,128]{5,3,4,2,1,0:T(8,128)(2,1)}), bf16[4,4,2,128,2,128]{5,3,4,2,1,0:T(8,128)(2,1)S(1)}, u32[]{:S(2)}, u32[]{:S(2)}) async-start(bf16[4,4,2,128,2,128]{5,3,4,2,1,0:T(8,128)(2,1)} %copy_select_fusion), calls=%async_computation.3 | async-start | bytes 4194304 | tf_op jit(solution)/shard_map/all_to_all | solution.py:108
  65.0 4.4 %fusion.1 = f32[64,2,8]{0,2,1:T(8,128)S(1)} fusion(f32[2,1792,64,8]{1,2,3,0:T(8,128)} %get-tuple-element.52, f32[64,2,8]{0,2,1:T(8,128)S(1)} %get-tuple-element.51), kind=kLoop, calls=%fused_computation.7 | loop fusion | flops 5504000 | bytes 7348224 | tf_op jit(solution)/shard_map/while/body/eval_jaxpr/reduce_sum | solution.py:58
  69.5 0.1 reshape_reshape_reshape.3
  69.7 2.0 %collective-permute-start = (f32[2,1,8,16]{3,2,0,1:T(8,128)S(1)}, f32[2,1,8,16]{3,2,0,1:T(8,128)S(1)}, u32[]{:S(2)}, u32[]{:S(2)}) collective-permute-start(f32[2,1,8,16]{3,2,0,1:T(8,128)S(1)} %bitcast.132), channel_id=1, source_target_pairs={{0,4},{4,0},{8,12},{12,8},{1,5},{5,1},{9,13},{13,9},{2,6},{6,2},{1... | collective-permute-start | bytes 3080 | tf_op jit(solution)/shard_map/ppermute | solution.py:26
  71.8 2.4 %collective-permute-start.1 = (f32[2,1,8,16]{3,2,0,1:T(8,128)S(1)}, f32[2,1,8,16]{3,2,0,1:T(8,128)S(1)}, u32[]{:S(2)}, u32[]{:S(2)}) collective-permute-start(f32[2,1,8,16]{3,2,0,1:T(8,128)S(1)} %bitcast.133), channel_id=1, source_target_pairs={{0,8},{4,12},{8,0},{12,4},{1,9},{5,13},{9,1},{13,5},{2,10},{6,14},... | collective-permute-start | bytes 3080 | tf_op jit(solution)/shard_map/ppermute | solution.py:26
  74.4 0.4 fusion.42
  74.9 0.2 convolution_bitcast_fusion.1
  75.4 0.6 dynamic-slice.16
  76.6 0.2 dynamic-update-slice
  76.9 22.8 %all-reduce = f32[32]{0:T(128)S(1)} all-reduce(f32[32]{0:T(128)S(1)} %dynamic-update-slice), channel_id=1, replica_groups=mesh['parts'=2,'dp'=4,'tensor'=4] {'dp'}, use_global_device_ids=true, to_apply=%add | all-reduce | flops 32 | bytes 256
  99.7 8.4 %collective-permute-done.1 = f32[2,1,8,16]{3,2,0,1:T(8,128)S(1)} collective-permute-done((f32[2,1,8,16]{3,2,0,1:T(8,128)S(1)}, f32[2,1,8,16]{3,2,0,1:T(8,128)S(1)}, u32[]{:S(2)}, u32[]{:S(2)}) %collective-permute-start.1) | collective-permute-done | bytes 1056 | tf_op jit(solution)/shard_map/ppermute | solution.py:26
  108.0 0.6 gather_fusion.2
  108.6 0.5 broadcast.239
  109.1 0.7 reduce.4
  109.9 1.3 multiply_reduce_fusion
  111.2 1.7 %gather_fusion.1 = bf16[8,2,128,2,128]{4,2,3,1,0:T(8,128)(2,1)} fusion(bf16[16,2,128,2,128]{4,2,3,1,0:T(8,128)(2,1)S(1)} %bitcast.127, s32[1024]{0:T(1024)S(1)} %pad_clamp_fusion.2), kind=kCustom, calls=%fused_computation.1 | custom fusion | bytes 2097184 | tf_op jit(solution)/shard_map/jit(_take)/gather | solution.py:109
  112.9 1.4 copy_select_fusion.1
  114.2 0.5 fusion.43
  114.7 0.3 convolution_bitcast_fusion
  115.0 0.2 fusion.16
  115.5 0.2 fusion.13
  115.7 0.1 multiply_reduce_fusion.1
  115.9 0.6 gather_fusion.3
  116.5 5.7 %psum.14 = f32[8]{0:T(128)S(1)} all-reduce(f32[8]{0:T(128)S(1)} %multiply_reduce_fusion.1), channel_id=1, replica_groups=mesh['parts'=2,'dp'=4,'tensor'=4] {'tensor'}, use_global_device_ids=true, to_apply=%region_12.13 | all-reduce | flops 8 | bytes 64 | tf_op jit(solution)/shard_map/psum | solution.py:166
  122.2 0.6 fusion.36
  122.8 12.7 %pmax.7 = f32[]{:T(128)} all-reduce(f32[]{:T(128)} %get-tuple-element.16), channel_id=1, replica_groups=mesh['parts'=2,'dp'=4,'tensor'=4] {'dp'}, use_global_device_ids=true, to_apply=%region_14.15 | all-reduce | flops 1 | bytes 8 | tf_op jit(solution)/shard_map/pmax | solution.py:168
  135.5 1.3 exponential_reduce_fusion
  136.8 9.1 %psum.15 = f32[]{:T(128)} all-reduce(f32[]{:T(128)} %exponential_reduce_fusion), channel_id=1, replica_groups=mesh['parts'=2,'dp'=4,'tensor'=4] {'dp'}, use_global_device_ids=true, to_apply=%region_16.17 | all-reduce | flops 1 | bytes 8 | tf_op jit(solution)/shard_map/psum | solution.py:169
  147.2 0.5 broadcast_subtract_fusion
  (57 shorter events, 1.3 us)
Async XLA Ops:
  0.6 50.4 %copy-start = (bf16[8,2,128,2,128]{4,3,2,1,0:T(2,128)(2,1)S(1)}, bf16[8,2,128,2,128]{4,3,2,1,0:T(2,128)(2,1)}, u32[]{:S(2)}) copy-start(bf16[8,2,128,2,128]{4,3,2,1,0:T(2,128)(2,1)} %param.8) | copy-start | bytes 3145732
  2.4 34.1 %all-to-all-start.2 = ((s32[4,1,4]{2,1,0:T(1,128)}), s32[4,1,4]{2,1,0:T(1,128)S(1)}, u32[]{:S(2)}, u32[]{:S(2)}) async-start(s32[4,1,4]{2,1,0:T(1,128)} %bitcast.10), calls=%async_computation.2 | async-start | bytes 4096 | tf_op jit(solution)/shard_map/all_to_all | solution.py:100
  36.4 10.4 %all-to-all-start.1 = ((f32[4,1,256]{2,1,0:T(1,128)}), f32[4,1,256]{2,1,0:T(1,128)S(1)}, u32[]{:S(2)}, u32[]{:S(2)}) async-start(f32[4,1,256]{2,1,0:T(1,128)} %reshape.278), calls=%async_computation.1 | async-start | bytes 8192 | tf_op jit(solution)/shard_map/all_to_all | solution.py:145
  46.9 14.5 %all-to-all-start = ((f32[2,4,8,16,128]{4,3,2,0,1:T(8,128)}), f32[2,4,8,16,128]{4,3,2,0,1:T(8,128)}, u32[]{:S(2)}, u32[]{:S(2)}) async-start(f32[2,4,8,16,128]{4,3,2,0,1:T(8,128)} %copy.88), calls=%async_computation | async-start | bytes 1048576 | tf_op jit(solution)/shard_map/all_to_all | solution.py:153
  56.2 18.2 %copy-start.3 = (bf16[2,2,8,2,128]{4,3,2,1,0:T(2,128)(2,1)S(1)}, bf16[2,2,8,2,128]{4,3,2,1,0:T(2,128)(2,1)}, u32[]{:S(2)}) copy-start(bf16[2,2,8,2,128]{4,3,2,1,0:T(2,128)(2,1)} %param.10) | copy-start | bytes 49156
  56.2 18.2 %copy-start.2 = (bf16[2,8,16,128]{3,2,1,0:T(8,128)(2,1)S(1)}, bf16[2,8,16,128]{3,2,1,0:T(8,128)(2,1)}, u32[]{:S(2)}) copy-start(bf16[2,8,16,128]{3,2,1,0:T(8,128)(2,1)} %param.9) | copy-start | bytes 196612
  57.9 17.5 %copy-start.7 = (u32[32]{0:T(128)S(1)}, u32[32]{0:T(128)}, u32[]{:S(2)}) copy-start(u32[32]{0:T(128)} %constant.120) | copy-start | bytes 388
  57.9 18.8 %copy-start.6 = (f32[8]{0:T(128)S(1)}, f32[8]{0:T(128)}, u32[]{:S(2)}) copy-start(f32[8]{0:T(128)} %param.12) | copy-start | bytes 100
  61.4 49.8 %all-to-all-start.3 = ((bf16[4,4,2,128,2,128]{5,3,4,2,1,0:T(8,128)(2,1)}), bf16[4,4,2,128,2,128]{5,3,4,2,1,0:T(8,128)(2,1)S(1)}, u32[]{:S(2)}, u32[]{:S(2)}) async-start(bf16[4,4,2,128,2,128]{5,3,4,2,1,0:T(8,128)(2,1)} %copy_select_fusion), calls=%async_computation.3 | async-start | bytes 4194304 | tf_op jit(solution)/shard_map/all_to_all | solution.py:108
  65.0 50.7 %copy-start.4 = (f32[16,128]{1,0:T(8,128)S(1)}, f32[16,128]{1,0:T(8,128)}, u32[]{:S(2)}) copy-start(f32[16,128]{1,0:T(8,128)} %param.13) | copy-start | bytes 24580
  65.0 57.2 %copy-start.5 = (s32[8]{0:T(128)S(1)}, s32[8]{0:T(128)}, u32[]{:S(2)}) copy-start(s32[8]{0:T(128)} %param.11) | copy-start | bytes 100
  69.7 29.9 %collective-permute-start = (f32[2,1,8,16]{3,2,0,1:T(8,128)S(1)}, f32[2,1,8,16]{3,2,0,1:T(8,128)S(1)}, u32[]{:S(2)}, u32[]{:S(2)}) collective-permute-start(f32[2,1,8,16]{3,2,0,1:T(8,128)S(1)} %bitcast.132), channel_id=1, source_target_pairs={{0,4},{4,0},{8,12},{12,8},{1,5},{5,1},{9,13},{13,9},{2,6},{6,2},{1... | collective-permute-start | bytes 3080 | tf_op jit(solution)/shard_map/ppermute | solution.py:26
  71.8 36.3 %collective-permute-start.1 = (f32[2,1,8,16]{3,2,0,1:T(8,128)S(1)}, f32[2,1,8,16]{3,2,0,1:T(8,128)S(1)}, u32[]{:S(2)}, u32[]{:S(2)}) collective-permute-start(f32[2,1,8,16]{3,2,0,1:T(8,128)S(1)} %bitcast.133), channel_id=1, source_target_pairs={{0,8},{4,12},{8,0},{12,4},{1,9},{5,13},{9,1},{13,5},{2,10},{6,14},... | collective-permute-start | bytes 3080 | tf_op jit(solution)/shard_map/ppermute | solution.py:26
  74.2 33.8 %collective-permute-start.2 = (f32[2,1,8,16]{3,2,0,1:T(8,128)S(1)}, f32[2,1,8,16]{3,2,0,1:T(8,128)S(1)}, u32[]{:S(2)}, u32[]{:S(2)}) collective-permute-start(f32[2,1,8,16]{3,2,0,1:T(8,128)S(1)} %bitcast.134), channel_id=1, source_target_pairs={{0,12},{4,8},{8,4},{12,0},{1,13},{5,9},{9,5},{13,1},{2,14},{6,10},... | collective-permute-start | bytes 3080 | tf_op jit(solution)/shard_map/ppermute | solution.py:26
  115.7 32.0 %copy-start.1 = (bf16[2,8,16,128]{3,2,1,0:T(8,128)(2,1)}, bf16[2,8,16,128]{3,2,1,0:T(8,128)(2,1)S(1)}, u32[]{:S(2)}) copy-start(bf16[2,8,16,128]{3,2,1,0:T(8,128)(2,1)S(1)} %fusion.13) | copy-start | bytes 196612
